TPU v7x, 32 devices: a whole 2x2x4 slice. The times are simulated.
32 devices in a mesh: tm: 2 (over y), aux: 16 (over z, x, core).
Axes of the slice: x: 2, y: 2, z: 4, core: 2. Of those that a mesh axis runs over, the one named last changes fastest.
Arguments:
- green: bfloat16 [4, 1024, 1024], P('tm'), may hold values from -4 to 4
- factors: bfloat16 [4096, 1024], P('aux'), may hold values from -0.1875 to 0.1875
- pattern: int32 [32, 8], P('aux'), may hold values 0 or 1
- coulomb: float32 [4096], P('aux'), may hold values from 0.5 to 2
Outputs:
- sigma: float32 [1024, 4, 1024], P('aux', 'tm')
All inputs are finite; a program needn't handle non-finite values. No bound on the sum of `pattern` on one device may be relied on, other than what follows from the above.
Results may differ from a plain program's by a relative error of at most 0.006.
Values may be sent and summed in bfloat16 or wider, within the bound.
A program may use at most 64 MiB of HBM per device.

v0:
```python
import functools

import jax
import jax.numpy as jnp
from jax import lax
from jax.experimental import pallas as pl
from jax.experimental.pallas import tpu as pltpu
from jax.sharding import PartitionSpec as P

MESH = pl.DeviceIdType.MESH
F32, BF16 = jnp.float32, jnp.bfloat16


def turned(p):
    return p + lax.div(p, 2) * (1 - 2 * lax.rem(p, 2))


def dot(a, b, da, db):
    return lax.dot_general(a, b, (((da,), (db,)), ((), ())), preferred_element_type=F32)


def kernel(cfg, pattern, factors, coul, green_hbm, out, own, rows, weights, green, left_right,
           own_right, cp, kern, sig, csend, crecv, xsend, xrecv, zsend, zrecv, fin,
           gsem, ring_s, ring_r, x_s, x_r, y_s, y_r, cc_s, cc_r, cx_s, cx_r,
           wring_s, wring_r, wx_s, wx_r, wcc_s, wcc_r, wcx_s, wcx_r, tm_s, tm_r,
           rc_s, rc_r, rx_s, rx_r, rz_s, rz_r):
    Z, X, JH, H = cfg
    T, O = green.shape[0], green.shape[1]
    R = own.shape[0]
    JW = O // JH
    OUT = out.shape[0]
    tms = lax.axis_size("tm")
    a, tmi = lax.axis_index("aux"), lax.axis_index("tm")
    c = lax.rem(a, 2)
    x = lax.rem(lax.div(a, 2), X)
    z = lax.div(a, 2 * X)
    pos = turned(z)

    def dev(z_, x_, c_):
        return (z_ * X + x_) * 2 + c_

    def xo(e):
        return lax.rem(x + e, X)

    def zo(f):
        return lax.rem(z + f, Z)

    partner = lax.rem(tmi + tms // 2, tms)
    plane = lax.rem(tmi, 2)
    mate = tmi + 1 - 2 * plane
    sibling = dev(z, x, 1 - c)
    sent = []

    def send(src, dst, s, r, **where):
        copy = pltpu.make_async_remote_copy(
            src_ref=src, dst_ref=dst, send_sem=s, recv_sem=r,
            device_id=where, device_id_type=MESH)
        copy.start()
        sent.append(copy)
        return copy

    loads = [pltpu.make_async_copy(green_hbm.at[t], green.at[t], gsem.at[t]) for t in range(T)]
    for copy in loads:
        copy.start()

    here = pl.multiple_of(a * R, R)
    brows = R // pattern.shape[0]
    bcols = O // pattern.shape[1]
    for i in range(pattern.shape[0]):
        for j in range(pattern.shape[1]):
            rs, cs = pl.ds(i * brows, brows), pl.ds(j * bcols, bcols)
            own[rs, cs] = (factors[rs, cs].astype(F32) * pattern[i, j].astype(F32)).astype(BF16)
    rows[pl.ds(here, R), :] = own[...]
    weights[a] = coul[...]
    cp[...] = jnp.transpose(jnp.broadcast_to(coul[...], (R, R)))

    barrier = pltpu.get_barrier_semaphore()
    friends = [{"aux": dev(zo(f), x, c)} for f in range(1, Z)]
    friends += [{"aux": dev(z, xo(e), c)} for e in range(1, X)]
    friends += [{"aux": sibling}, {"tm": partner}]
    if tms > 2 and tms % 2 == 0:
        friends += [{"tm": mate}]
    for where in friends:
        pl.semaphore_signal(barrier, inc=1, device_id=where, device_id_type=MESH)
    pl.semaphore_wait(barrier, len(friends))

    nextd = dev(turned(lax.rem(pos + 1, Z)), x, c)
    PR = R // H
    shared = (1,) if tms % 2 == 0 else ()

    def col_owner(k):
        return dev(turned(lax.rem(pos + Z - k, Z)), x, c)

    def xin_owner(k, e):
        return dev(turned(lax.rem(pos + Z - k, Z)), lax.rem(x + X - e, X), c)

    def pass_piece(owner, h, s, r, first=False, **where):
        at = pl.ds(pl.multiple_of(owner * R + h * PR, PR), PR)
        src = own.at[pl.ds(pl.multiple_of(h * PR, PR), PR)] if first else rows.at[at]
        return send(src, rows.at[at], s, r, **where)

    def pass_weight(owner, s, r, first=False, **where):
        return send(coul if first else weights.at[owner], weights.at[owner], s, r, **where)

    ring, xs, ys, ccs, cxs = {}, {}, {}, {}, {}
    wring, wxs, wccs, wcxs = {}, {}, {}, {}

    def wait_all(copies):
        for copy in copies:
            copy.wait_recv()

    def col(k, h):
        if k > 0:
            ring[k, h].wait_recv()
            if h == 0:
                wring[k].wait_recv()
        owner, first = col_owner(k), k == 0
        if k < Z - 1:
            ring[k + 1, h] = pass_piece(owner, h, ring_s.at[k, h], ring_r.at[k, h], first, aux=nextd)
        for e in range(1, X):
            to = dev(z, xo(e), c)
            if k not in shared:
                xs[k, e, h] = pass_piece(owner, h, x_s.at[k, e - 1, h], x_r.at[k, e - 1, h], first,
                                         aux=to)
            elif h % 2:
                i = h // 2
                xs[k, e, i] = pass_piece(owner, 2 * i + plane, x_s.at[k, e - 1, i],
                                         x_r.at[k, e - 1, i], first, aux=to)
        ccs.setdefault(k, []).append(
            pass_piece(owner, h, cc_s.at[k, h], cc_r.at[k, h], first, aux=sibling))
        if h == 0:
            if k < Z - 1:
                wring[k + 1] = pass_weight(owner, wring_s.at[k], wring_r.at[k], first, aux=nextd)
            for e in range(1, X):
                wxs[k, e] = pass_weight(owner, wx_s.at[k, e - 1], wx_r.at[k, e - 1], first,
                                        aux=dev(z, xo(e), c))
            ccs[k].append(pass_weight(owner, wcc_s.at[k], wcc_r.at[k], first, aux=sibling))

    def xin(k, i):
        for e in range(1, X):
            owner = xin_owner(k, e)
            xs[k, e, i].wait_recv()
            h, n = i, i
            if k in shared:
                h, n = 2 * i + plane, 2 * i
                ys[k, e, i] = pass_piece(owner, h, y_s.at[k, e - 1, i], y_r.at[k, e - 1, i], tm=mate)
            mine = cxs.setdefault((k, e), [])
            mine.append(pass_piece(owner, h, cx_s.at[k, e - 1, n], cx_r.at[k, e - 1, n], aux=sibling))
            if i == 0:
                wxs[k, e].wait_recv()
                mine.append(pass_weight(owner, wcx_s.at[k, e - 1], wcx_r.at[k, e - 1], aux=sibling))

    def yin(k, i):
        for e in range(1, X):
            ys[k, e, i].wait_recv()
            cxs[k, e].append(
                pass_piece(xin_owner(k, e), 2 * i + 1 - plane, cx_s.at[k, e - 1, 2 * i + 1],
                           cx_r.at[k, e - 1, 2 * i + 1], aux=sibling))

    waited = set()

    def once(key, copies):
        if key not in waited:
            waited.add(key)
            wait_all(copies)

    def blocks(owner, ts):
        def one(i, carry):
            who = owner - c + lax.rem(c + lax.div(i, len(ts)), 2)
            t = ts[0] + lax.rem(i, len(ts))
            at = pl.ds(pl.multiple_of(who * R, R), R)
            both = dot(left_right[t], rows[at, :], 1, 1)
            ag, mirror = both[:R], both[R:]
            kern[t, :, at] = (ag * ag * mirror * (cp[...] * weights[who])).astype(BF16)
            return carry
        lax.fori_loop(0, 2 * len(ts), one, 0)

    def do_col(k, ts):
        once(("c", k), ccs[k])
        blocks(col_owner(k), ts)

    def do_xin(k, ts):
        for e in range(1, X):
            once(("x", k, e), cxs[k, e])
            blocks(xin_owner(k, e), ts)

    rights = {}

    def project_right(t):
        loads[t].wait()

        def one(j, carry):
            at = pl.ds(pl.multiple_of(j * 256, 256), 256)
            own_right[t, :, at] = dot(own[...], green[t, at, :], 1, 1).astype(BF16)
            return carry
        lax.fori_loop(0, O // 256, one, 0)
        rights[t] = send(own_right.at[t], left_right.at[t, pl.ds(R, R)], tm_s.at[t], tm_r.at[t],
                         tm=partner)

    def project_left(t):
        def one(j, carry):
            at = pl.ds(pl.multiple_of(j * 256, 256), 256)
            left_right[t, pl.ds(0, R), at] = dot(own[...], green[t, :, at], 1, 0).astype(BF16)
            return carry
        lax.fori_loop(0, O // 256, one, 0)

    for h in range(H):
        col(0, h)
    for t in range(T):
        project_right(t)
    for t in range(T):
        project_left(t)

    rest, every = tuple(range(1, T)), tuple(range(T))
    todo = []

    def plan(when, what, *args):
        todo.append((when, len(todo), what, args))

    lag = 0.7
    for k in range(1, Z):
        for h in range(H):
            plan((k - 1) * H + h + 1 + lag * k, col, k, h)
    last = 0.0
    for k in range(Z):
        if k in shared:
            for i in range(H // 2):
                ready = (k - 1) * H + 2 * i + 2 + lag * k
                last = max(last + 1, ready + 1 + lag)
                plan(last, xin, k, i)
                plan(max(last + 1 + lag, 11.7 + i), yin, k, i)
        else:
            for i in range(H):
                last = k * H + i + 1 + lag
                plan(last, xin, k, i)
    plan(6.5, lambda: rights[0].wait_recv())
    plan(6.6, do_col, 0, (0,))
    plan(6.7, do_col, 1, (0,))
    plan(6.8, do_xin, 0, (0,))
    plan(13.3, do_xin, 1, (0,))
    plan(9.6, do_col, 2, (0,))
    plan(10.6, lambda: [rights[t].wait_recv() for t in rest])
    plan(10.61, do_col, 0, rest)
    plan(10.8, do_col, 1, rest)
    plan(11.2, do_xin, 0, rest)
    plan(13.35, do_xin, 1, rest)
    plan(12.3, do_col, 2, rest)
    tail = 13.3
    for k in range(2, Z):
        if k > 2:
            plan(max(tail, (k - 1) * H + H + lag * k + 0.5), do_col, k, every)
        full = max([w for w, _, f, g in todo if f in (xin, yin) and g[0] == k])
        plan(full + 0.4, do_xin, k, every)
    for _, _, what, args in sorted(todo, key=lambda item: item[:2]):
        what(*args)

    pairs = Z * X
    cross, xc, zc = {}, {}, {}

    def stage_a(q):
        t, j0 = q // JH, (q % JH) * JW

        def one(j, carry):
            at = pl.ds(pl.multiple_of(j0 + j * 256, 256), 256)
            carried = dot(kern[t], rows[:, at], 1, 0).astype(BF16)
            to = pl.ds(pl.multiple_of(j * 256, 256), 256)
            sig[q, :, to] = dot(own[...], carried, 0, 0)
            return carry
        lax.fori_loop(0, JW // 256, one, 0)
        for g in range(pairs):
            at = pl.ds(pl.multiple_of((g * 2 + 1 - c) * OUT, OUT), OUT)
            csend[q, g] = sig[q, at, :].astype(BF16)
        cross[q] = send(csend.at[q], crecv.at[q], rc_s.at[q], rc_r.at[q], aux=sibling)

    def summed(q, g):
        at = pl.ds(pl.multiple_of((g * 2 + c) * OUT, OUT), OUT)
        return sig[q, at, :] + crecv[q, g].astype(F32)

    def stage_b(q):
        cross[q].wait_recv()
        for e in range(1, X):
            for zz in range(Z):
                xsend[q, e - 1, zz] = summed(q, zz * X + xo(e)).astype(BF16)
            xc[q, e] = send(xsend.at[q, e - 1], xrecv.at[q, e - 1], rx_s.at[q, e - 1],
                            rx_r.at[q, e - 1], aux=dev(z, xo(e), c))

    def stage_c(q):
        for e in range(1, X):
            xc[q, e].wait_recv()
        for f in list(range(1, Z)) + [0]:
            value = summed(q, zo(f) * X + x)
            for e in range(1, X):
                value = value + xrecv[q, e - 1, zo(f)].astype(F32)
            if f == 0:
                fin[q] = value
            else:
                zsend[q, f - 1] = value.astype(BF16)
                zc[q, f] = send(zsend.at[q, f - 1], zrecv.at[q, f - 1], rz_s.at[q, f - 1],
                                rz_r.at[q, f - 1], aux=dev(zo(f), x, c))

    def stage_d(q):
        value = fin[q]
        for f in range(1, Z):
            zc[q, f].wait_recv()
            value = value + zrecv[q, f - 1].astype(F32)
        out[:, q // JH, pl.ds((q % JH) * JW, JW)] = value

    Q = T * JH
    todo.clear()
    step, hop = 10.4 / Q, 22.5 / Q
    for q in range(Q):
        plan(step * (q + 1), stage_a, q)
        plan(step * (q + 2) + 0.1, stage_b, q)
        arrived = 2 * step + 1 + hop * (q + 1) + 1.5
        plan(arrived, stage_c, q)
        plan(arrived + hop + 2.5, stage_d, q)
    for _, _, what, args in sorted(todo, key=lambda item: item[:2]):
        what(*args)
    for copy in sent:
        copy.wait_send()


def local(green, factors, pattern, coulomb):
    n = lax.axis_size("aux")
    T, O, _ = green.shape
    R = factors.shape[0]
    A = n * R
    chips = n // 2
    Z = 4
    X = chips // Z
    JH = 2
    H = 4
    JW = O // JH
    Q = T * JH
    OUT = O // n
    dma = pltpu.SemaphoreType.DMA
    vm = pltpu.VMEM
    scratch = [
        vm((R, O), BF16), vm((A, O), BF16), vm((n, 1, R), F32), vm((T, O, O), BF16),
        vm((T, 2 * R, O), BF16), vm((T, R, O), BF16), vm((R, R), F32), vm((T, R, A), BF16),
        vm((Q, O, JW), F32), vm((Q, chips, OUT, JW), BF16), vm((Q, chips, OUT, JW), BF16),
        vm((Q, X - 1, Z, OUT, JW), BF16), vm((Q, X - 1, Z, OUT, JW), BF16),
        vm((Q, Z - 1, OUT, JW), BF16), vm((Q, Z - 1, OUT, JW), BF16), vm((Q, OUT, JW), F32),
        dma((T,)),
        dma((Z - 1, H)), dma((Z - 1, H)),
        dma((Z, X - 1, H)), dma((Z, X - 1, H)),
        dma((Z, X - 1, H // 2)), dma((Z, X - 1, H // 2)),
        dma((Z, H)), dma((Z, H)),
        dma((Z, X - 1, H)), dma((Z, X - 1, H)),
        dma((Z - 1,)), dma((Z - 1,)), dma((Z, X - 1)), dma((Z, X - 1)),
        dma((Z,)), dma((Z,)), dma((Z, X - 1)), dma((Z, X - 1)),
        dma((T,)), dma((T,)),
        dma((Q,)), dma((Q,)),
        dma((Q, X - 1)), dma((Q, X - 1)),
        dma((Q, Z - 1)), dma((Q, Z - 1)),
    ]
    vmem = pl.BlockSpec(memory_space=pltpu.VMEM)
    result = pl.pallas_call(
        functools.partial(kernel, (Z, X, JH, H)),
        out_shape=jax.ShapeDtypeStruct((OUT, T, O), F32),
        in_specs=[pl.BlockSpec(memory_space=pltpu.SMEM), vmem, vmem,
                  pl.BlockSpec(memory_space=pl.ANY)],
        out_specs=vmem,
        scratch_shapes=scratch,
        compiler_params=pltpu.CompilerParams(
            collective_id=0, has_side_effects=True, vmem_limit_bytes=60 * 2**20),
    )(pattern, factors, coulomb.reshape(1, R), green)
    return result


def solution(mesh):
    in_specs = (P("tm", None, None), P("aux", None), P("aux", None), P("aux"))
    out_specs = P("aux", "tm", None)
    return jax.shard_map(local, mesh=mesh, in_specs=in_specs, out_specs=out_specs, check_vma=False)
```

profile of v0, /device:TPU:0, one launch (start us, length us, event | category | flops | bytes accessed | tf_op | source)
XLA Modules:
  0.0 92.6 jit_solution(17698554664118775520)
XLA Ops:
  0.0 90.7 %shard_map.46 = f32[64,2,1024]{2,1,0:T(2,128)} custom-call(s32[2,8]{1,0:T(2,128)} %pattern.1, bf16[256,1024]{1,0:T(8,128)(2,1)} %factors.1, f32[1,256]{1,0:T(1,128)} %bitcast.1, bf16[2,1024,1024]{2,1,0:T(8,128)(2,1)} %green_hbm.1), custom_call_target="tpu_custom_call" | custom-call | tf_op jit(solution)/shard_map/pallas_call | solution.py:358
  90.7 1.9 %copy.6 = f32[64,2,1024]{2,1,0:T(2,128)} copy(f32[64,2,1024]{2,1,0:T(2,128)} %shard_map.46) | data formatting | bytes 1048576
where the time goes:
time: 92.7 us; the launch traced here: 92.6 us
  Pallas kernels  90.7 us (98%)
  local copies, waits for them, and re-layouts  1.87 us (2%)
    pallas_call x1, Pallas kernels, local(): pl.pallas_call(functools.partial(kernel, (Z, X, JH, H)), out_shape=jax.Sh...  90.7 us
    unnamed x1, local copies, waits for them, and re-layouts  1.87 us

commit v1 on v0

v1 whole, which is shorter than its diff:
```python
import functools

import jax
import jax.numpy as jnp
from jax import lax
from jax.experimental import pallas as pl
from jax.experimental.pallas import tpu as pltpu
from jax.sharding import PartitionSpec as P

MESH = pl.DeviceIdType.MESH
F32, BF16 = jnp.float32, jnp.bfloat16


def turned(p):
    return p + lax.div(p, 2) * (1 - 2 * lax.rem(p, 2))


def dot(a, b, da, db):
    return lax.dot_general(a, b, (((da,), (db,)), ((), ())), preferred_element_type=F32)


def kernel(cfg, pattern, factors, coul, halves, green_hbm, out,
           pm, rows, weights, pweights, green, psend, lhs, cp, kern, car, sig,
           csend, crecv, xsend, xrecv, zsend, zrecv,
           gsem, z_s, z_r, y_s, y_r, b_s, b_r, s_s, s_r, w_s, w_r, pw_s, pw_r,
           m_s, m_r, p_s, p_r, f_s, f_r, rc_s, rc_r, rx_s, rx_r, rz_s, rz_r):
    Z, X, HP = cfg
    T, O = green.shape[0], green.shape[1]
    U = T // 2
    R2 = pm.shape[2]
    R = 2 * R2
    PR = R2 // HP
    OUT = out.shape[1]
    CH = 2 * X * OUT
    tms = lax.axis_size("tm")
    a, tmi = lax.axis_index("aux"), lax.axis_index("tm")
    c = lax.rem(a, 2)
    x = lax.rem(lax.div(a, 2), X)
    z = lax.div(a, 2 * X)
    pos = turned(z)
    upper = lax.div(tmi, tms // 2)
    partner = lax.rem(tmi + tms // 2, tms)
    plane = lax.rem(tmi, 2)
    mate = tmi + 1 - 2 * plane

    def dev(z_, x_, c_):
        return (z_ * X + x_) * 2 + c_

    def xo(e):
        return lax.rem(x + e, X)

    def zo(f):
        return lax.rem(z + f, Z)

    def ring(k):
        return turned(lax.rem(pos + k, Z))

    sibling = dev(z, x, 1 - c)
    nextd = dev(ring(1), x, c)
    sent = []

    def send(src, dst, s, r, **where):
        copy = pltpu.make_async_remote_copy(
            src_ref=src, dst_ref=dst, send_sem=s, recv_sem=r,
            device_id=where, device_id_type=MESH)
        copy.start()
        sent.append(copy)
        return copy

    def slot(j):
        return (1 - upper) * U + j if j < U else upper * U + j - U

    loads = [pltpu.make_async_copy(green_hbm.at[slot(j)], green.at[j], gsem.at[j]) for j in range(T)]
    for copy in loads:
        copy.start()

    barrier = pltpu.get_barrier_semaphore()
    friends = [{"aux": dev(zo(f), x, c)} for f in range(1, Z)]
    friends += [{"aux": dev(zo(f), x, 1 - c)} for f in range(Z)]
    friends += [{"aux": dev(z, xo(e), c)} for e in range(1, X)]
    friends += [{"aux": dev(zo(f), x, c), "tm": partner} for f in range(Z)]
    if tms > 2:
        friends += [{"tm": mate}]
    for where in friends:
        pl.semaphore_signal(barrier, inc=1, device_id=where, device_id_type=MESH)

    brows = R // pattern.shape[0]
    bcols = O // pattern.shape[1]
    step = min(brows, R2)
    for r0 in range(0, R, step):
        for j in range(pattern.shape[1]):
            rs, cs = pl.ds(r0, step), pl.ds(j * bcols, bcols)
            part = (factors[rs, cs].astype(F32) * pattern[r0 // brows, j].astype(F32)).astype(BF16)
            to = pl.ds(r0 % R2, step)
            pm[0, r0 // R2, to, cs] = part
            rows[0, r0 // R2, 0, to, cs] = part
    weights[0, 0] = halves[...]
    pweights[0] = coul[...]
    pl.semaphore_wait(barrier, len(friends))

    def cut(i):
        return pl.ds(i * PR, PR)

    zc, yc, sc, wc, pwc, mc, pc, fc = {}, {}, {}, {}, {}, {}, {}, {}

    for i in range(HP):
        zc[1, 0, i] = send(pm.at[0, plane, cut(i)], rows.at[1, plane, 0, cut(i)],
                           z_s.at[1, 0, i], z_r.at[1, 0, i], aux=nextd)
    for e in range(1, X):
        for h in range(2):
            mc[e, h] = send(pm.at[0, h], pm.at[X - e, h], m_s.at[e, h], m_r.at[e, h],
                            aux=dev(z, xo(e), c))
    for h in range(2):
        sc[0, h, 0] = send(pm.at[0, h], rows.at[0, h, 1], s_s.at[0, h, 0], s_r.at[0, h, 0], aux=sibling)
    for e in range(1, X):
        pwc[e] = send(coul, pweights.at[X - e], pw_s.at[e], pw_r.at[e], aux=dev(z, xo(e), c))
    for k in range(Z):
        for s in range(2):
            if k + s:
                wc[k, s] = send(halves, weights.at[k, s], w_s.at[k, s], w_r.at[k, s],
                                aux=dev(ring(k), x, c + s * (1 - 2 * c)))

    def project(g, e, store):
        def run(first):
            def one(j, carry):
                at = pl.ds(pl.multiple_of(j * 256, 256), 256)
                m = pm[e].reshape(R, O)
                if first:
                    value = dot(m, green[g, :, at], 1, 0)
                else:
                    value = dot(m, green[g, at, :], 1, 1)
                store(at, value.astype(BF16))
                return carry
            lax.fori_loop(0, O // 256, one, 0)

        pl.when(upper == 0)(lambda: run(True))
        pl.when(upper == 1)(lambda: run(False))

    def to_partner(u):
        loads[u].wait()

        def store(at, value):
            psend[u, 0, :, at] = value[:R2]
            psend[u, 1, :, at] = value[R2:]
        project(u, 0, store)
        for h in range(2):
            for i in range(HP):
                pc[u, h, i] = send(psend.at[u, h, cut(i)], lhs.at[u, h, upper, cut(i)],
                                   p_s.at[u, h, i], p_r.at[u, h, i], tm=partner)

    def keep(u, e):
        def store(at, value):
            lhs[u, 2 * e, upper, :, at] = value[:R2]
            lhs[u, 2 * e + 1, upper, :, at] = value[R2:]
        project(U + u, e, store)

    for u in range(U):
        to_partner(u)
    for u in range(U):
        loads[U + u].wait()
        keep(u, 0)

    def half_of(w):
        return plane if w == 0 else 1 - plane

    def across(k, w, i):
        half = half_of(w)
        sc[k, w, i] = send(rows.at[k, half, 0, cut(i)], rows.at[k, half, 1, cut(i)],
                           s_s.at[k, w, i], s_r.at[k, w, i], aux=sibling)

    def forward(k, w, i):
        half = half_of(w)
        zc[k + 1, w, i] = send(rows.at[k, half, 0, cut(i)], rows.at[k + 1, half, 0, cut(i)],
                               z_s.at[k + 1, w, i], z_r.at[k + 1, w, i], aux=nextd)

    def share(k, i):
        yc[k, i] = send(rows.at[k, plane, 0, cut(i)], rows.at[k, plane, 0, cut(i)],
                        y_s.at[k, i], y_r.at[k, i], tm=mate)

    def on_z(k, w, i, share_now=True):
        zc[k, w, i].wait_recv()
        if k < Z - 1:
            forward(k, w, i)
            if share_now:
                share(k, i)
        across(k, w, i)

    def on_y(k, i):
        yc[k, i].wait_recv()
        if k == Z - 2:
            forward(k, 1, i)
        across(k, 1, i)

    def on_p(u, h, i):
        pc[u, h, i].wait_recv()
        for e in range(1, X):
            at = lhs.at[u, h, 1 - upper, cut(i)]
            fc[u, e, h, i] = send(at, lhs.at[u, 2 * (X - e) + h, 1 - upper, cut(i)],
                                  f_s.at[u, e, h, i], f_r.at[u, e, h, i], aux=dev(z, xo(e), c))

    waited = set()

    def once(*copies):
        for copy in copies:
            if id(copy) not in waited:
                waited.add(id(copy))
                copy.wait_recv()

    def set_cp(e):
        cp[2 * e] = jnp.transpose(jnp.broadcast_to(pweights[e], (R, R)))[:R2]
        cp[2 * e + 1] = jnp.transpose(jnp.broadcast_to(pweights[e], (R, R)))[R2:]

    def others(e):
        for h in range(2):
            once(mc[e, h])
        once(pwc[e])
        set_cp(e)
        for u in range(U):
            keep(u, e)

    def need(k, w):
        if k == 0:
            once(sc[0, w, 0])
        else:
            for i in range(HP):
                once(sc[k, w, i])
        for s in range(2):
            if k + s:
                once(wc[k, s])

    def tiles(p0, pn, k, w):
        need(k, w)
        half = w if k == 0 else half_of(w)
        at = pl.ds(pl.multiple_of((k * 2 + half) * R, R), R)
        g = min(pn, 2)

        def one(n, carry):
            u, p = lax.div(n, pn // g), p0 + g * lax.rem(n, pn // g)
            both = dot(lhs[u, pl.ds(p, g)].reshape(g * R, O), rows[k, half].reshape(R, O), 1, 1)
            wq = jnp.concatenate([weights[k, 0, half], weights[k, 1, half]], axis=1)
            for i in range(g):
                ax, bx = both[i * R:i * R + R2], both[i * R + R2:(i + 1) * R]
                w_ = ax * bx * (cp[p + i] * wq)
                to = pl.ds(pl.multiple_of((p + i) * R2, R2), R2)
                kern[u, 0, to, at] = (w_ * ax).astype(BF16)
                kern[u, 1, to, at] = (w_ * bx).astype(BF16)
            return carry
        lax.fori_loop(0, U * (pn // g), one, 0)

    todo = []

    def plan(when, what, *args):
        todo.append((when, len(todo), what, args))

    def run_plan():
        for _, _, what, args in sorted(todo, key=lambda item: item[:2]):
            what(*args)
        todo.clear()

    PT, L = 5.6 / HP, 1.6
    for i in range(HP):
        plan(PT * (i + 1) + L, on_z, 1, 0, i, False)
        plan(5.6 + PT * (i + 1) + L, on_z, 2, 0, i)
        plan(11.2 + PT * (i + 1) + L, on_z, 3, 0, i)
        plan(16.8 + PT * (i + 1) + L, on_z, 3, 1, i)
        plan(12.8 + PT * (i + 1) + L + 0.1, on_y, 2, i)
        plan(18.4 + PT * (i + 1) + L, on_y, 1, i)
        plan(5.6 + PT * HP + L + 0.05, share, 1, i)
        for h in range(2):
            plan(0.8 + (5.6 * h + PT * (i + 1)) + L + 0.05, lambda h, i: [on_p(u, h, i) for u in range(U)], h, i)
    for e in range(1, X):
        plan(13.0, others, e)
    plan(1.0, set_cp, 0)
    t0 = 13.9
    plan(t0, tiles, 0, 2, 0, 0)
    plan(t0, tiles, 0, 2, 0, 1)
    plan(t0 + 0.3, tiles, 0, 2, 1, 0)
    plan(t0 + 1.5, tiles, 0, 2, 2, 0)
    plan(19.8, tiles, 0, 2, 3, 0)
    plan(20.7, tiles, 0, 2, 2, 1)

    def got(h):
        for u in range(U):
            for e in range(1, X):
                for i in range(HP):
                    once(fc[u, e, h, i])

    def rest(h, units):
        got(h)
        for e in range(1, X):
            for k, w in units:
                tiles(2 * e + h, 1, k, w)
    plan(18.9, rest, 0, [(0, 0), (0, 1), (1, 0), (2, 0)])
    plan(22.7, rest, 0, [(3, 0), (2, 1)])
    early = [(0, 0), (0, 1), (1, 0), (2, 0), (3, 0), (2, 1)]
    plan(24.7, rest, 1, early)
    plan(26.0, tiles, 0, 2 * X, 3, 1)
    plan(26.6, tiles, 0, 2 * X, 1, 1)
    run_plan()

    def carried(u, typ, at):
        return dot(kern[u, typ], rows[:, :, :, :, at].reshape(Z * 2 * R, 256), 1, 0).astype(BF16)

    def all_carried(u):
        def one(j, carry):
            at = pl.ds(pl.multiple_of(j * 256, 256), 256)
            car[u, :, at] = carried(u, 0, at)
            return carry
        lax.fori_loop(0, O // 256, one, 0)

    cross, xc, zs = {}, {}, {}

    def stage_a(q, u, typ, f):
        at = pl.ds(pl.multiple_of(zo(f) * CH, CH), CH)
        if typ:
            def part(n, carry):
                cols = pl.ds(pl.multiple_of(n * 256, 256), 256)
                src = pl.ds(pl.multiple_of(zo(f) * CH + n * 256, 256), 256)
                car[U, :, cols] = carried(u, 1, src)
                return carry
            lax.fori_loop(0, CH // 256, part, 0)

        def one(j, carry):
            to = pl.ds(pl.multiple_of(j * 512, 512), 512)
            if typ:
                value = dot(car[U, :, pl.ds(0, CH)], pm[:, :, :, to].reshape(X * R, 512), 0, 0)
            else:
                value = dot(pm[:, :, :, at].reshape(X * R, CH), car[u, :, to], 0, 0)
            sig[q, :, to] = value
            return carry
        lax.fori_loop(0, O // 512, one, 0)
        for g in range(X):
            mine = pl.ds(pl.multiple_of((g * 2 + 1 - c) * OUT, OUT), OUT)
            csend[q, g] = sig[q, mine, :].astype(BF16)
        cross[q] = send(csend.at[q], crecv.at[q], rc_s.at[q], rc_r.at[q], aux=sibling)

    def summed(q, g):
        at = pl.ds(pl.multiple_of((g * 2 + c) * OUT, OUT), OUT)
        return sig[q, at, :] + crecv[q, g].astype(F32)

    def stage_b(q):
        cross[q].wait_recv()
        for e in range(1, X):
            xsend[q, e - 1] = summed(q, xo(e)).astype(BF16)
            xc[q, e] = send(xsend.at[q, e - 1], xrecv.at[q, e - 1], rx_s.at[q, e - 1],
                            rx_r.at[q, e - 1], aux=dev(z, xo(e), c))

    def last(u, typ, f, tm):
        return pltpu.make_async_remote_copy(
            src_ref=zsend.at[u, typ, f], dst_ref=zrecv.at[upper, u, f],
            send_sem=rz_s.at[u, typ, f], recv_sem=rz_r.at[upper, u, f],
            device_id={"aux": dev(zo(f), x, c), "tm": tm}, device_id_type=MESH)

    def stage_c(q, u, typ, f):
        for e in range(1, X):
            xc[q, e].wait_recv()
        value = summed(q, x)
        for e in range(1, X):
            value = value + xrecv[q, e - 1].astype(F32)
        away = (upper - typ) * (upper - typ)
        if f:
            zsend[u, typ, f] = value.astype(BF16)
            copy = last(u, typ, f, tmi + (partner - tmi) * away)
            copy.start()
            sent.append(copy)
        else:
            @pl.when(away == 0)
            def _():
                zrecv[upper, u, 0] = value.astype(BF16)

            @pl.when(away == 1)
            def _():
                zsend[u, typ, 0] = value.astype(BF16)
                last(u, typ, 0, partner).start()

    def stage_d(sh, u):
        value = None
        for f in [2, 1, 3, 0][-Z:]:
            copy = pltpu.make_async_remote_copy(
                src_ref=zsend.at[u, 0, f], dst_ref=zrecv.at[sh, u, f],
                send_sem=rz_s.at[u, 0, f], recv_sem=rz_r.at[sh, u, f],
                device_id={"tm": partner}, device_id_type=MESH)
            if f:
                copy.wait_recv()
            else:
                pl.when(upper != sh)(copy.wait_recv)
            piece = zrecv[sh, u, f].astype(F32)
            value = piece if value is None else value + piece
        out[sh * U + u] = value

    order = [(u, typ, f) for u in range(U) for f in [2, 1, 3, 0] for typ in (1, 0)]
    compute, hop = 0.9, 22.5 / len(order)
    at = 0.0
    for q, (u, typ, f) in enumerate(order):
        if f == 2 and typ == 0:
            plan(at, all_carried, u)
            at += 2.2
        at += compute
        plan(at, stage_a, q, u, typ, f)
        b = at + 1.7
        plan(b, stage_b, q)
        arrived = max(b, compute + 1.7 + hop * q) + hop + 1.8
        plan(arrived, stage_c, q, u, typ, f)
    for u in range(U):
        plan(100.0, stage_d, 0, u)
        plan(100.0, stage_d, 1, u)
    run_plan()
    for copy in sent:
        copy.wait_send()
    for u in range(U):
        for typ in range(2):
            pl.when(upper != typ)(last(u, typ, 0, partner).wait_send)


def local(green, factors, pattern, coulomb):
    n = lax.axis_size("aux")
    T, O, _ = green.shape
    R = factors.shape[0]
    chips = n // 2
    Z = 4
    X = chips // Z
    HP = 2
    R2 = R // 2
    U = T // 2
    OUT = O // n
    CH = 2 * X * OUT
    Q = U * 2 * Z
    dma = pltpu.SemaphoreType.DMA
    vm = pltpu.VMEM
    scratch = [
        vm((X, 2, R2, O), BF16), vm((Z, 2, 2, R2, O), BF16), vm((Z, 2, 2, 1, R2), F32),
        vm((X, 1, R), F32), vm((T, O, O), BF16), vm((U, 2, R2, O), BF16),
        vm((U, 2 * X, 2, R2, O), BF16), vm((2 * X, R2, R), F32),
        vm((U, 2, X * R, Z * 2 * R), BF16), vm((U + 1, X * R, O), BF16), vm((Q, CH, O), F32),
        vm((Q, X, OUT, O), BF16), vm((Q, X, OUT, O), BF16),
        vm((Q, X - 1, OUT, O), BF16), vm((Q, X - 1, OUT, O), BF16),
        vm((U, 2, Z, OUT, O), BF16), vm((2, U, Z, OUT, O), BF16),
        dma((T,)),
        dma((Z, 2, HP)), dma((Z, 2, HP)), dma((Z, HP)), dma((Z, HP)),
        dma((1,)), dma((1,)),
        dma((Z, 2, HP)), dma((Z, 2, HP)), dma((Z, 2)), dma((Z, 2)), dma((X,)), dma((X,)),
        dma((X, 2)), dma((X, 2)), dma((U, 2, HP)), dma((U, 2, HP)),
        dma((U, X, 2, HP)), dma((U, X, 2, HP)),
        dma((Q,)), dma((Q,)), dma((Q, X - 1)), dma((Q, X - 1)),
        dma((U, 2, Z)), dma((2, U, Z)),
    ]
    vmem = pl.BlockSpec(memory_space=pltpu.VMEM)
    result = pl.pallas_call(
        functools.partial(kernel, (Z, X, HP)),
        out_shape=jax.ShapeDtypeStruct((T, OUT, O), F32),
        in_specs=[pl.BlockSpec(memory_space=pltpu.SMEM), vmem, vmem, vmem,
                  pl.BlockSpec(memory_space=pl.ANY)],
        out_specs=vmem,
        scratch_shapes=scratch,
        compiler_params=pltpu.CompilerParams(
            collective_id=0, has_side_effects=True, vmem_limit_bytes=60 * 2**20),
    )(pattern, factors, coulomb.reshape(1, R), coulomb.reshape(2, 1, R2), green)
    return jnp.transpose(result, (1, 0, 2))


def solution(mesh):
    in_specs = (P("tm", None, None), P("aux", None), P("aux", None), P("aux"))
    out_specs = P("aux", "tm", None)
    return jax.shard_map(local, mesh=mesh, in_specs=in_specs, out_specs=out_specs, check_vma=False)
```

time: 92.7 us -> 76.9 us (0.83)
  Pallas kernels: 90.7 us -> 74.4 us
    pallas_call x1, Pallas kernels: 90.7 us -> 74.4 us  [local(): pl.pallas_call(functools.partial(kernel, (Z, X, HP)), out_shape=jax.Shape...]
    transpose x0 -> x1, local copies, waits for them, and re-layouts: none -> 2.24 us  [local(): return jnp.transpose(result, (1, 0, 2))]
    unnamed x1 -> x0, local copies, waits for them, and re-layouts: 1.87 us -> none
where the time goes in v1:
time: 76.9 us; the launch traced here: 76.7 us
  Pallas kernels  74.4 us (97%)
  local copies, waits for them, and re-layouts  2.24 us (3%)
    pallas_call x1, Pallas kernels, local(): pl.pallas_call(functools.partial(kernel, (Z, X, HP)), out_shape=jax.Shape...  74.4 us
    transpose x1, local copies, waits for them, and re-layouts, local(): return jnp.transpose(result, (1, 0, 2))  2.24 us

profile of v1, /device:TPU:0, one launch (start us, length us, event | category | flops | bytes accessed | tf_op | source)
XLA Modules:
  0.0 76.7 jit_solution(9390100117898711817)
XLA Ops:
  0.0 74.4 %shard_map.46 = f32[2,64,1024]{2,1,0:T(8,128)} custom-call(s32[2,8]{1,0:T(2,128)} %pattern.1, bf16[256,1024]{1,0:T(8,128)(2,1)} %factors.1, f32[1,256]{1,0:T(1,128)} %bitcast.4, f32[2,1,128]{2,1,0:T(1,128)} %bitcast.5, bf16[2,1024,1024]{2,1,0:T(8,128)(2,1)} %green_hbm.1), custom_call_target="tpu_custom_call" | custom-call | tf_op jit(solution)/shard_map/pallas_call | solution.py:448
  74.4 2.2 %copy.5 = f32[64,2,1024]{2,1,0:T(2,128)} copy(f32[64,2,1024]{2,0,1:T(8,128)} %bitcast.3) | data formatting | bytes 1048576 | tf_op jit(solution)/shard_map/transpose | solution.py:458

commit v2 on v1

--- a/solution.py
+++ b/solution.py
@@ -20,10 +20,11 @@
 
 
 def kernel(cfg, pattern, factors, coul, halves, green_hbm, out,
-           pm, rows, weights, pweights, green, psend, lhs, cp, kern, car, sig,
-           csend, crecv, xsend, xrecv, zsend, zrecv,
-           gsem, z_s, z_r, y_s, y_r, b_s, b_r, s_s, s_r, w_s, w_r, pw_s, pw_r,
-           m_s, m_r, p_s, p_r, f_s, f_r, rc_s, rc_r, rx_s, rx_r, rz_s, rz_r):
+           pm, rows, weights, pweights, green, psend, lhs, cp, kern, car, acc, sig,
+           csend, crecv, xsend, xrecv, zsend, zrecv, nrecv, gsend, grecv, tsend, trecv, fin,
+           gsem, z_s, z_r, y_s, y_r, s_s, s_r, w_s, w_r, pw_s, pw_r,
+           m_s, m_r, p_s, p_r, f_s, f_r, rc_s, rc_r, rx_s, rx_r, rz_s, rz_r,
+           rn_s, rn_r, rg_s, rg_r, rt_s, rt_r):
     Z, X, HP = cfg
     T, O = green.shape[0], green.shape[1]
     U = T // 2
@@ -78,7 +79,7 @@
     friends = [{"aux": dev(zo(f), x, c)} for f in range(1, Z)]
     friends += [{"aux": dev(zo(f), x, 1 - c)} for f in range(Z)]
     friends += [{"aux": dev(z, xo(e), c)} for e in range(1, X)]
-    friends += [{"aux": dev(zo(f), x, c), "tm": partner} for f in range(Z)]
+    friends += [{"tm": partner}]
     if tms > 2:
         friends += [{"tm": mate}]
     for where in friends:
@@ -120,21 +121,14 @@
                 wc[k, s] = send(halves, weights.at[k, s], w_s.at[k, s], w_r.at[k, s],
                                 aux=dev(ring(k), x, c + s * (1 - 2 * c)))
 
-    def project(g, e, store):
-        def run(first):
-            def one(j, carry):
-                at = pl.ds(pl.multiple_of(j * 256, 256), 256)
-                m = pm[e].reshape(R, O)
-                if first:
-                    value = dot(m, green[g, :, at], 1, 0)
-                else:
-                    value = dot(m, green[g, at, :], 1, 1)
-                store(at, value.astype(BF16))
-                return carry
-            lax.fori_loop(0, O // 256, one, 0)
-
-        pl.when(upper == 0)(lambda: run(True))
-        pl.when(upper == 1)(lambda: run(False))
+    def project(g, e, turn, store):
+        def one(j, carry):
+            at = pl.ds(pl.multiple_of(j * 256, 256), 256)
+            m = pm[e].reshape(R, O)
+            value = dot(m, green[g, at, :], 1, 1) if turn else dot(m, green[g, :, at], 1, 0)
+            store(at, value.astype(BF16))
+            return carry
+        lax.fori_loop(0, O // 256, one, 0)
 
     def to_partner(u):
         loads[u].wait()
@@ -142,17 +136,17 @@
         def store(at, value):
             psend[u, 0, :, at] = value[:R2]
             psend[u, 1, :, at] = value[R2:]
-        project(u, 0, store)
+        project(u, 0, True, store)
         for h in range(2):
             for i in range(HP):
-                pc[u, h, i] = send(psend.at[u, h, cut(i)], lhs.at[u, h, upper, cut(i)],
+                pc[u, h, i] = send(psend.at[u, h, cut(i)], lhs.at[u, h, 1, cut(i)],
                                    p_s.at[u, h, i], p_r.at[u, h, i], tm=partner)
 
     def keep(u, e):
         def store(at, value):
-            lhs[u, 2 * e, upper, :, at] = value[:R2]
-            lhs[u, 2 * e + 1, upper, :, at] = value[R2:]
-        project(U + u, e, store)
+            lhs[u, 2 * e, 0, :, at] = value[:R2]
+            lhs[u, 2 * e + 1, 0, :, at] = value[R2:]
+        project(U + u, e, False, store)
 
     for u in range(U):
         to_partner(u)
@@ -194,8 +188,7 @@
     def on_p(u, h, i):
         pc[u, h, i].wait_recv()
         for e in range(1, X):
-            at = lhs.at[u, h, 1 - upper, cut(i)]
-            fc[u, e, h, i] = send(at, lhs.at[u, 2 * (X - e) + h, 1 - upper, cut(i)],
+            fc[u, e, h, i] = send(lhs.at[u, h, 1, cut(i)], lhs.at[u, 2 * (X - e) + h, 1, cut(i)],
                                   f_s.at[u, e, h, i], f_r.at[u, e, h, i], aux=dev(z, xo(e), c))
 
     waited = set()
@@ -246,6 +239,22 @@
                 kern[u, 1, to, at] = (w_ * bx).astype(BF16)
             return carry
         lax.fori_loop(0, U * (pn // g), one, 0)
+
+    def early_carried(u, typ):
+        def one(j, carry):
+            at = pl.ds(pl.multiple_of(j * 256, 256), 256)
+            value = None
+            for k in range(Z):
+                if k in (0, 2):
+                    mine, part = pl.ds(2 * k * R, 2 * R), rows[k, :, :, :, at].reshape(2 * R, 256)
+                else:
+                    mine = pl.ds(pl.multiple_of((k * 2 + plane) * R, R), R)
+                    part = rows[k, plane, :, :, at].reshape(R, 256)
+                term = dot(kern[u, typ, pl.ds(0, R), mine], part, 1, 0)
+                value = term if value is None else value + term
+            acc[u, typ, :, at] = value
+            return carry
+        lax.fori_loop(0, O // 256, one, 0)
 
     todo = []
 
@@ -279,6 +288,10 @@
     plan(19.8, tiles, 0, 2, 3, 0)
     plan(20.7, tiles, 0, 2, 2, 1)
 
+    for u in range(U):
+        plan(21.4, early_carried, u, 1)
+        plan(21.4 + 0.9, early_carried, u, 0)
+
     def got(h):
         for u in range(U):
             for e in range(1, X):
@@ -298,118 +311,126 @@
     plan(26.6, tiles, 0, 2 * X, 1, 1)
     run_plan()
 
-    def carried(u, typ, at):
-        return dot(kern[u, typ], rows[:, :, :, :, at].reshape(Z * 2 * R, 256), 1, 0).astype(BF16)
-
-    def all_carried(u):
-        def one(j, carry):
-            at = pl.ds(pl.multiple_of(j * 256, 256), 256)
-            car[u, :, at] = carried(u, 0, at)
-            return carry
-        lax.fori_loop(0, O // 256, one, 0)
-
-    cross, xc, zs = {}, {}, {}
-
-    def stage_a(q, u, typ, f):
-        at = pl.ds(pl.multiple_of(zo(f) * CH, CH), CH)
+    def column(k, half):
+        return pl.ds(pl.multiple_of((k * 2 + half) * R, R), R)
+
+    def carried(u, typ, at, width):
+        late = 1 - plane
+        near = acc[u, typ, :, at]
+        for k in (1, Z - 1):
+            near = near + dot(kern[u, typ, pl.ds(0, R), column(k, late)], rows[k, late, :, :, at].reshape(R, width), 1, 0)
+        far = dot(kern[u, typ, pl.ds(R, (X - 1) * R)], rows[:, :, :, :, at].reshape(Z * 2 * R, width), 1, 0)
+        return jnp.concatenate([near.astype(BF16), far.astype(BF16)], axis=0)
+
+    def block(u, n):
+        width = O // 4
+        at = pl.ds(n * width, width)
+        car[u, :, at] = carried(u, 0, at, width)
+
+    DIAG, CROSS, NB, OWN = range(4)
+    ZF, DIRECT = (1,), ()
+    nbz = z + 1 - 2 * lax.rem(z, 2)
+    target = [lax.rem(nbz + 2, Z), zo(2), nbz, z]
+    nbd, crossd = dev(nbz, x, c), dev(zo(2), x, c)
+    cross, xc, nc, gc, zf, tc = {}, {}, {}, {}, {}, {}
+
+    def index(u, typ, d):
+        return (u * 2 + typ) * 4 + d
+
+    def stage_a(u, typ, d):
+        q = index(u, typ, d)
+        base = target[d] * CH
+        at = pl.ds(pl.multiple_of(base, CH), CH)
         if typ:
-            def part(n, carry):
-                cols = pl.ds(pl.multiple_of(n * 256, 256), 256)
-                src = pl.ds(pl.multiple_of(zo(f) * CH + n * 256, 256), 256)
-                car[U, :, cols] = carried(u, 1, src)
-                return carry
-            lax.fori_loop(0, CH // 256, part, 0)
-
-        def one(j, carry):
-            to = pl.ds(pl.multiple_of(j * 512, 512), 512)
-            if typ:
-                value = dot(car[U, :, pl.ds(0, CH)], pm[:, :, :, to].reshape(X * R, 512), 0, 0)
-            else:
-                value = dot(pm[:, :, :, at].reshape(X * R, CH), car[u, :, to], 0, 0)
-            sig[q, :, to] = value
-            return carry
-        lax.fori_loop(0, O // 512, one, 0)
+            car[U, :, pl.ds(0, CH)] = carried(u, 1, at, CH)
+            sig[q] = dot(car[U, :, pl.ds(0, CH)], pm[...].reshape(X * R, O), 0, 0)
+        else:
+            sig[q] = dot(pm[:, :, :, at].reshape(X * R, CH), car[u], 0, 0)
         for g in range(X):
             mine = pl.ds(pl.multiple_of((g * 2 + 1 - c) * OUT, OUT), OUT)
             csend[q, g] = sig[q, mine, :].astype(BF16)
         cross[q] = send(csend.at[q], crecv.at[q], rc_s.at[q], rc_r.at[q], aux=sibling)
 
-    def summed(q, g):
+    def summed(u, typ, d, g):
+        q = index(u, typ, d)
         at = pl.ds(pl.multiple_of((g * 2 + c) * OUT, OUT), OUT)
-        return sig[q, at, :] + crecv[q, g].astype(F32)
-
-    def stage_b(q):
-        cross[q].wait_recv()
+        value = sig[q, at, :] + crecv[q, g].astype(F32)
+        if d == OWN and typ in ZF:
+            value = value + grecv[u, typ, g].astype(F32)
+        return value
+
+    def stage_g(u, typ, part):
+        once(cross[index(u, typ, NB)])
+        for g in range(X):
+            if g * 2 // X == part:
+                gsend[u, typ, g] = summed(u, typ, NB, g).astype(BF16)
+                gc[u, typ, g] = send(gsend.at[u, typ, g], grecv.at[u, typ, g], rg_s.at[u, typ, g],
+                                     rg_r.at[u, typ, g], aux=nbd)
+
+    def stage_b(u, typ, d):
+        q = index(u, typ, d)
+        once(cross[q])
+        if d == OWN and typ in ZF:
+            once(*[gc[u, typ, g] for g in range(X)])
         for e in range(1, X):
-            xsend[q, e - 1] = summed(q, xo(e)).astype(BF16)
+            xsend[q, e - 1] = summed(u, typ, d, xo(e)).astype(BF16)
             xc[q, e] = send(xsend.at[q, e - 1], xrecv.at[q, e - 1], rx_s.at[q, e - 1],
                             rx_r.at[q, e - 1], aux=dev(z, xo(e), c))
 
-    def last(u, typ, f, tm):
-        return pltpu.make_async_remote_copy(
-            src_ref=zsend.at[u, typ, f], dst_ref=zrecv.at[upper, u, f],
-            send_sem=rz_s.at[u, typ, f], recv_sem=rz_r.at[upper, u, f],
-            device_id={"aux": dev(zo(f), x, c), "tm": tm}, device_id_type=MESH)
-
-    def stage_c(q, u, typ, f):
+    def stage_c(u, typ, d):
+        q = index(u, typ, d)
         for e in range(1, X):
-            xc[q, e].wait_recv()
-        value = summed(q, x)
+            once(xc[q, e])
+        value = summed(u, typ, d, x)
         for e in range(1, X):
             value = value + xrecv[q, e - 1].astype(F32)
-        away = (upper - typ) * (upper - typ)
-        if f:
-            zsend[u, typ, f] = value.astype(BF16)
-            copy = last(u, typ, f, tmi + (partner - tmi) * away)
-            copy.start()
-            sent.append(copy)
+        if d == CROSS and typ not in DIRECT:
+            once(nc[u, typ])
+            value = value + nrecv[u, typ].astype(F32)
+        if d == OWN:
+            fin[u, typ] = value
+            return
+        zsend[q] = value.astype(BF16)
+        if d == DIAG and typ in DIRECT:
+            zf[u, typ, 2] = send(zsend.at[q], zrecv.at[u, typ, 2], rz_s.at[u, typ, 2],
+                                 rz_r.at[u, typ, 2], aux=dev(target[DIAG], x, c))
+        elif d == DIAG:
+            nc[u, typ] = send(zsend.at[q], nrecv.at[u, typ], rn_s.at[u, typ], rn_r.at[u, typ], aux=nbd)
         else:
-            @pl.when(away == 0)
-            def _():
-                zrecv[upper, u, 0] = value.astype(BF16)
-
-            @pl.when(away == 1)
-            def _():
-                zsend[u, typ, 0] = value.astype(BF16)
-                last(u, typ, 0, partner).start()
-
-    def stage_d(sh, u):
-        value = None
-        for f in [2, 1, 3, 0][-Z:]:
-            copy = pltpu.make_async_remote_copy(
-                src_ref=zsend.at[u, 0, f], dst_ref=zrecv.at[sh, u, f],
-                send_sem=rz_s.at[u, 0, f], recv_sem=rz_r.at[sh, u, f],
-                device_id={"tm": partner}, device_id_type=MESH)
-            if f:
-                copy.wait_recv()
-            else:
-                pl.when(upper != sh)(copy.wait_recv)
-            piece = zrecv[sh, u, f].astype(F32)
-            value = piece if value is None else value + piece
-        out[sh * U + u] = value
-
-    order = [(u, typ, f) for u in range(U) for f in [2, 1, 3, 0] for typ in (1, 0)]
-    compute, hop = 0.9, 22.5 / len(order)
-    at = 0.0
-    for q, (u, typ, f) in enumerate(order):
-        if f == 2 and typ == 0:
-            plan(at, all_carried, u)
-            at += 2.2
-        at += compute
-        plan(at, stage_a, q, u, typ, f)
-        b = at + 1.7
-        plan(b, stage_b, q)
-        arrived = max(b, compute + 1.7 + hop * q) + hop + 1.8
-        plan(arrived, stage_c, q, u, typ, f)
+            to = 0 if d == NB else 1
+            zf[u, typ, to] = send(zsend.at[q], zrecv.at[u, typ, to], rz_s.at[u, typ, to],
+                                  rz_r.at[u, typ, to], aux=nbd if d == NB else crossd)
+
+    def stage_d(u, typ):
+        value = fin[u, typ]
+        for to in (2, 1, 0):
+            if (to == 0 and typ not in ZF) or to == 1 or (to == 2 and typ in DIRECT):
+                once(zf[u, typ, to])
+                value = value + zrecv[u, typ, to].astype(F32)
+        if typ:
+            tsend[u] = value.astype(BF16)
+            tc[u] = send(tsend.at[u], trecv.at[u], rt_s.at[u], rt_r.at[u], tm=partner)
+        else:
+            out[upper * U + u] = value
+
+    def stage_e(u):
+        once(tc[u])
+        out[(1 - upper) * U + u] = trecv[u].astype(F32)
+
+    steps = (
+        ("A", 1, DIAG), ("A", 1, NB), ("B", 1, DIAG), ("A", 1, CROSS), ("G", 1, 0), ("W", 0),
+        ("B", 1, CROSS), ("W", 1), ("W", 2), ("W", 3), ("A", 0, DIAG), ("C", 1, DIAG),
+        ("G", 1, 1), ("A", 0, CROSS), ("B", 0, DIAG), ("A", 1, OWN), ("B", 0, CROSS), ("A", 0, NB),
+        ("C", 1, CROSS), ("A", 0, OWN), ("B", 1, OWN), ("B", 0, NB), ("C", 0, DIAG), ("C", 0, CROSS),
+        ("B", 0, OWN), ("C", 1, OWN), ("D", 1), ("C", 0, NB), ("C", 0, OWN), ("E",),
+        ("D", 0),
+    )
+    run = {"A": stage_a, "B": stage_b, "C": stage_c, "D": stage_d, "E": stage_e, "G": stage_g, "W": block}
     for u in range(U):
-        plan(100.0, stage_d, 0, u)
-        plan(100.0, stage_d, 1, u)
-    run_plan()
+        for step in steps:
+            run[step[0]](u, *step[1:])
     for copy in sent:
         copy.wait_send()
-    for u in range(U):
-        for typ in range(2):
-            pl.when(upper != typ)(last(u, typ, 0, partner).wait_send)
 
 
 def local(green, factors, pattern, coulomb):
@@ -431,18 +452,20 @@
         vm((X, 2, R2, O), BF16), vm((Z, 2, 2, R2, O), BF16), vm((Z, 2, 2, 1, R2), F32),
         vm((X, 1, R), F32), vm((T, O, O), BF16), vm((U, 2, R2, O), BF16),
         vm((U, 2 * X, 2, R2, O), BF16), vm((2 * X, R2, R), F32),
-        vm((U, 2, X * R, Z * 2 * R), BF16), vm((U + 1, X * R, O), BF16), vm((Q, CH, O), F32),
+        vm((U, 2, X * R, Z * 2 * R), BF16), vm((U + 1, X * R, O), BF16), vm((U, 2, R, O), F32), vm((Q, CH, O), F32),
         vm((Q, X, OUT, O), BF16), vm((Q, X, OUT, O), BF16),
         vm((Q, X - 1, OUT, O), BF16), vm((Q, X - 1, OUT, O), BF16),
-        vm((U, 2, Z, OUT, O), BF16), vm((2, U, Z, OUT, O), BF16),
+        vm((Q, OUT, O), BF16), vm((U, 2, 3, OUT, O), BF16), vm((U, 2, OUT, O), BF16),
+        vm((U, 2, X, OUT, O), BF16), vm((U, 2, X, OUT, O), BF16),
+        vm((U, OUT, O), BF16), vm((U, OUT, O), BF16), vm((U, 2, OUT, O), F32),
         dma((T,)),
         dma((Z, 2, HP)), dma((Z, 2, HP)), dma((Z, HP)), dma((Z, HP)),
-        dma((1,)), dma((1,)),
         dma((Z, 2, HP)), dma((Z, 2, HP)), dma((Z, 2)), dma((Z, 2)), dma((X,)), dma((X,)),
         dma((X, 2)), dma((X, 2)), dma((U, 2, HP)), dma((U, 2, HP)),
         dma((U, X, 2, HP)), dma((U, X, 2, HP)),
         dma((Q,)), dma((Q,)), dma((Q, X - 1)), dma((Q, X - 1)),
-        dma((U, 2, Z)), dma((2, U, Z)),
+        dma((U, 2, 3)), dma((U, 2, 3)), dma((U, 2)), dma((U, 2)),
+        dma((U, 2, X)), dma((U, 2, X)), dma((U,)), dma((U,)),
     ]
     vmem = pl.BlockSpec(memory_space=pltpu.VMEM)
     result = pl.pallas_call(

time: 76.9 us -> 70 us (0.910)
  Pallas kernels: 74.4 us -> 67.6 us
    pallas_call x1, Pallas kernels: 74.4 us -> 67.6 us  [local(): pl.pallas_call(functools.partial(kernel, (Z, X, HP)), out_shape=jax.Shape...]
where the time goes in v2:
time: 70 us; the launch traced here: 69.8 us
  Pallas kernels  67.6 us (97%)
  local copies, waits for them, and re-layouts  2.24 us (3%)
    pallas_call x1, Pallas kernels, local(): pl.pallas_call(functools.partial(kernel, (Z, X, HP)), out_shape=jax.Shape...  67.6 us
    transpose x1, local copies, waits for them, and re-layouts, local(): return jnp.transpose(result, (1, 0, 2))  2.24 us

profile of v2, /device:TPU:0, one launch (start us, length us, event | category | flops | bytes accessed | tf_op | source)
XLA Modules:
  0.0 69.8 jit_solution(16305820197138126287)
XLA Ops:
  0.0 67.6 %shard_map.46 = f32[2,64,1024]{2,1,0:T(8,128)} custom-call(s32[2,8]{1,0:T(2,128)} %pattern.1, bf16[256,1024]{1,0:T(8,128)(2,1)} %factors.1, f32[1,256]{1,0:T(1,128)} %bitcast.4, f32[2,1,128]{2,1,0:T(1,128)} %bitcast.5, bf16[2,1024,1024]{2,1,0:T(8,128)(2,1)} %green_hbm.1), custom_call_target="tpu_custom_call" | custom-call | tf_op jit(solution)/shard_map/pallas_call | solution.py:471
  67.6 2.2 %copy.5 = f32[64,2,1024]{2,1,0:T(2,128)} copy(f32[64,2,1024]{2,0,1:T(8,128)} %bitcast.3) | data formatting | bytes 1048576 | tf_op jit(solution)/shard_map/transpose | solution.py:481

commit v3 on v2

--- a/solution.py
+++ b/solution.py
@@ -19,10 +19,10 @@
     return lax.dot_general(a, b, (((da,), (db,)), ((), ())), preferred_element_type=F32)
 
 
-def kernel(cfg, pattern, factors, coul, halves, green_hbm, out,
-           pm, rows, weights, pweights, green, psend, lhs, cp, kern, car, acc, sig,
+def kernel(cfg, pattern_hbm, factors_hbm, coul_hbm, halves_hbm, green_hbm, out_hbm,
+           pattern, factors, out,           pm, rows, weights, pweights, green, psend, lhs, cp, kern, car, acc, sig,
            csend, crecv, xsend, xrecv, zsend, zrecv, nrecv, gsend, grecv, tsend, trecv, fin,
-           gsem, z_s, z_r, y_s, y_r, s_s, s_r, w_s, w_r, pw_s, pw_r,
+           gsem, isem, osem, z_s, z_r, y_s, y_r, s_s, s_r, w_s, w_r, pw_s, pw_r,
            m_s, m_r, p_s, p_r, f_s, f_r, rc_s, rc_r, rx_s, rx_r, rz_s, rz_r,
            rn_s, rn_r, rg_s, rg_r, rt_s, rt_r):
     Z, X, HP = cfg
@@ -72,9 +72,6 @@
         return (1 - upper) * U + j if j < U else upper * U + j - U
 
     loads = [pltpu.make_async_copy(green_hbm.at[slot(j)], green.at[j], gsem.at[j]) for j in range(T)]
-    for copy in loads:
-        copy.start()
-
     barrier = pltpu.get_barrier_semaphore()
     friends = [{"aux": dev(zo(f), x, c)} for f in range(1, Z)]
     friends += [{"aux": dev(zo(f), x, 1 - c)} for f in range(Z)]
@@ -84,6 +81,13 @@
         friends += [{"tm": mate}]
     for where in friends:
         pl.semaphore_signal(barrier, inc=1, device_id=where, device_id_type=MESH)
+    inputs = [(pattern_hbm, pattern), (factors_hbm, factors), (coul_hbm, pweights.at[0]),
+              (halves_hbm, weights.at[0, 0])]
+    inputs = [pltpu.make_async_copy(src, dst, isem.at[n]) for n, (src, dst) in enumerate(inputs)]
+    for copy in inputs + loads:
+        copy.start()
+    for copy in inputs:
+        copy.wait()
 
     brows = R // pattern.shape[0]
     bcols = O // pattern.shape[1]
@@ -95,8 +99,6 @@
             to = pl.ds(r0 % R2, step)
             pm[0, r0 // R2, to, cs] = part
             rows[0, r0 // R2, 0, to, cs] = part
-    weights[0, 0] = halves[...]
-    pweights[0] = coul[...]
     pl.semaphore_wait(barrier, len(friends))
 
     def cut(i):
@@ -114,11 +116,11 @@
     for h in range(2):
         sc[0, h, 0] = send(pm.at[0, h], rows.at[0, h, 1], s_s.at[0, h, 0], s_r.at[0, h, 0], aux=sibling)
     for e in range(1, X):
-        pwc[e] = send(coul, pweights.at[X - e], pw_s.at[e], pw_r.at[e], aux=dev(z, xo(e), c))
+        pwc[e] = send(pweights.at[0], pweights.at[X - e], pw_s.at[e], pw_r.at[e], aux=dev(z, xo(e), c))
     for k in range(Z):
         for s in range(2):
             if k + s:
-                wc[k, s] = send(halves, weights.at[k, s], w_s.at[k, s], w_r.at[k, s],
+                wc[k, s] = send(weights.at[0, 0], weights.at[k, s], w_s.at[k, s], w_r.at[k, s],
                                 aux=dev(ring(k), x, c + s * (1 - 2 * c)))
 
     def project(g, e, turn, store):
@@ -401,6 +403,13 @@
             zf[u, typ, to] = send(zsend.at[q], zrecv.at[u, typ, to], rz_s.at[u, typ, to],
                                   rz_r.at[u, typ, to], aux=nbd if d == NB else crossd)
 
+    ends = []
+
+    def finish(n, t):
+        copy = pltpu.make_async_copy(out.at[t], out_hbm.at[t], osem.at[n])
+        copy.start()
+        ends.append(copy)
+
     def stage_d(u, typ):
         value = fin[u, typ]
         for to in (2, 1, 0):
@@ -412,17 +421,19 @@
             tc[u] = send(tsend.at[u], trecv.at[u], rt_s.at[u], rt_r.at[u], tm=partner)
         else:
             out[upper * U + u] = value
+            finish(u, upper * U + u)
 
     def stage_e(u):
         once(tc[u])
         out[(1 - upper) * U + u] = trecv[u].astype(F32)
+        finish(U + u, (1 - upper) * U + u)
 
     steps = (
         ("A", 1, DIAG), ("A", 1, NB), ("B", 1, DIAG), ("A", 1, CROSS), ("G", 1, 0), ("W", 0),
         ("B", 1, CROSS), ("W", 1), ("W", 2), ("W", 3), ("A", 0, DIAG), ("C", 1, DIAG),
-        ("G", 1, 1), ("A", 0, CROSS), ("B", 0, DIAG), ("A", 1, OWN), ("B", 0, CROSS), ("A", 0, NB),
-        ("C", 1, CROSS), ("A", 0, OWN), ("B", 1, OWN), ("B", 0, NB), ("C", 0, DIAG), ("C", 0, CROSS),
-        ("B", 0, OWN), ("C", 1, OWN), ("D", 1), ("C", 0, NB), ("C", 0, OWN), ("E",),
+        ("G", 1, 1), ("A", 0, CROSS), ("B", 0, DIAG), ("B", 0, CROSS), ("A", 1, OWN), ("A", 0, NB),
+        ("C", 1, CROSS), ("B", 0, NB), ("A", 0, OWN), ("B", 1, OWN), ("C", 0, DIAG), ("C", 0, CROSS),
+        ("B", 0, OWN), ("C", 0, NB), ("C", 1, OWN), ("D", 1), ("C", 0, OWN), ("E",),
         ("D", 0),
     )
     run = {"A": stage_a, "B": stage_b, "C": stage_c, "D": stage_d, "E": stage_e, "G": stage_g, "W": block}
@@ -431,6 +442,8 @@
             run[step[0]](u, *step[1:])
     for copy in sent:
         copy.wait_send()
+    for copy in ends:
+        copy.wait()
 
 
 def local(green, factors, pattern, coulomb):
@@ -449,6 +462,7 @@
     dma = pltpu.SemaphoreType.DMA
     vm = pltpu.VMEM
     scratch = [
+        pltpu.SMEM(pattern.shape, jnp.int32), vm((R, O), BF16), vm((T, OUT, O), F32),
         vm((X, 2, R2, O), BF16), vm((Z, 2, 2, R2, O), BF16), vm((Z, 2, 2, 1, R2), F32),
         vm((X, 1, R), F32), vm((T, O, O), BF16), vm((U, 2, R2, O), BF16),
         vm((U, 2 * X, 2, R2, O), BF16), vm((2 * X, R2, R), F32),
@@ -458,7 +472,7 @@
         vm((Q, OUT, O), BF16), vm((U, 2, 3, OUT, O), BF16), vm((U, 2, OUT, O), BF16),
         vm((U, 2, X, OUT, O), BF16), vm((U, 2, X, OUT, O), BF16),
         vm((U, OUT, O), BF16), vm((U, OUT, O), BF16), vm((U, 2, OUT, O), F32),
-        dma((T,)),
+        dma((T,)), dma((4,)), dma((T,)),
         dma((Z, 2, HP)), dma((Z, 2, HP)), dma((Z, HP)), dma((Z, HP)),
         dma((Z, 2, HP)), dma((Z, 2, HP)), dma((Z, 2)), dma((Z, 2)), dma((X,)), dma((X,)),
         dma((X, 2)), dma((X, 2)), dma((U, 2, HP)), dma((U, 2, HP)),
@@ -467,16 +481,14 @@
         dma((U, 2, 3)), dma((U, 2, 3)), dma((U, 2)), dma((U, 2)),
         dma((U, 2, X)), dma((U, 2, X)), dma((U,)), dma((U,)),
     ]
-    vmem = pl.BlockSpec(memory_space=pltpu.VMEM)
     result = pl.pallas_call(
         functools.partial(kernel, (Z, X, HP)),
         out_shape=jax.ShapeDtypeStruct((T, OUT, O), F32),
-        in_specs=[pl.BlockSpec(memory_space=pltpu.SMEM), vmem, vmem, vmem,
-                  pl.BlockSpec(memory_space=pl.ANY)],
-        out_specs=vmem,
+        in_specs=[pl.BlockSpec(memory_space=pl.ANY)] * 5,
+        out_specs=pl.BlockSpec(memory_space=pl.ANY),
         scratch_shapes=scratch,
         compiler_params=pltpu.CompilerParams(
-            collective_id=0, has_side_effects=True, vmem_limit_bytes=60 * 2**20),
+            collective_id=0, has_side_effects=True, vmem_limit_bytes=53 * 2**20),
     )(pattern, factors, coulomb.reshape(1, R), coulomb.reshape(2, 1, R2), green)
     return jnp.transpose(result, (1, 0, 2))
 

time: 70 us -> 67.7 us (0.967)
  Pallas kernels: 67.6 us -> 65 us
    pallas_call x1, Pallas kernels: 67.6 us -> 65 us  [local(): pl.pallas_call(functools.partial(kernel, (Z, X, HP)), out_shape=jax.Shape...]
    unnamed x0 -> x4, local copies, waits for them, and re-layouts: none -> 1.36 us
    transpose x1, local copies, waits for them, and re-layouts: 2.24 us -> 1.2 us  [local(): return jnp.transpose(result, (1, 0, 2))]
where the time goes in v3:
time: 67.7 us; the launch traced here: 67.5 us
  Pallas kernels  65 us (96%)
  local copies, waits for them, and re-layouts  2.56 us (4%)
    pallas_call x1, Pallas kernels, local(): pl.pallas_call(functools.partial(kernel, (Z, X, HP)), out_shape=jax.Shape...  65 us
    unnamed x4, local copies, waits for them, and re-layouts  1.36 us

profile of v3, /device:TPU:0, one launch (start us, length us, event | category | flops | bytes accessed | tf_op | source)
XLA Modules:
  0.0 67.5 jit_solution(1803152069006082783)
XLA Ops:
  0.0 0.0 copy-start
  0.0 0.7 %copy-done = f32[256]{0:T(256)S(1)} copy-done((f32[256]{0:T(256)S(1)}, f32[256]{0:T(256)}, u32[]{:S(2)}) %copy-start) | copy-done | bytes 1048
  0.7 0.0 copy-start.1
  0.7 0.7 %copy-done.1 = s32[2,8]{1,0:T(2,128)S(1)} copy-done((s32[2,8]{1,0:T(2,128)S(1)}, s32[2,8]{1,0:T(2,128)}, u32[]{:S(2)}) %copy-start.1) | copy-done | bytes 88
  1.4 65.0 %shard_map.46 = f32[2,64,1024]{2,1,0:T(8,128)S(1)} custom-call(s32[2,8]{1,0:T(2,128)S(1)} %copy-done.1, bf16[256,1024]{1,0:T(8,128)(2,1)} %factors_hbm.1, f32[1,256]{1,0:T(1,128)S(1)} %bitcast.4, f32[2,1,128]{2,1,0:T(1,128)S(1)} %bitcast.5, bf16[2,1024,1024]{2,1,0:T(8,128)(2,1)} %green_hbm.1), custom_call_target="tpu_custom_call" | custom-call | tf_op jit(solution)/shard_map/pallas_call | solution.py:484
  66.3 1.2 %copy.5 = f32[64,2,1024]{2,1,0:T(2,128)} copy(f32[64,2,1024]{2,0,1:T(8,128)S(1)} %bitcast.3) | data formatting | bytes 1048576 | tf_op jit(solution)/shard_map/transpose | solution.py:493
Async XLA Ops:
  0.0 0.7 %copy-start = (f32[256]{0:T(256)S(1)}, f32[256]{0:T(256)}, u32[]{:S(2)}) copy-start(f32[256]{0:T(256)} %param.7) | copy-start | bytes 3076
  0.7 0.7 %copy-start.1 = (s32[2,8]{1,0:T(2,128)S(1)}, s32[2,8]{1,0:T(2,128)}, u32[]{:S(2)}) copy-start(s32[2,8]{1,0:T(2,128)} %pattern_hbm.1) | copy-start | bytes 196

commit v4 on v3

--- a/solution.py
+++ b/solution.py
@@ -20,7 +20,7 @@
 
 
 def kernel(cfg, pattern_hbm, factors_hbm, coul_hbm, halves_hbm, green_hbm, out_hbm,
-           pattern, factors, out,           pm, rows, weights, pweights, green, psend, lhs, cp, kern, car, acc, sig,
+           pattern, factors, out,           pm, rows, weights, pweights, green, psend, lhs, cp, kern, car, sig,
            csend, crecv, xsend, xrecv, zsend, zrecv, nrecv, gsend, grecv, tsend, trecv, fin,
            gsem, isem, osem, z_s, z_r, y_s, y_r, s_s, s_r, w_s, w_r, pw_s, pw_r,
            m_s, m_r, p_s, p_r, f_s, f_r, rc_s, rc_r, rx_s, rx_r, rz_s, rz_r,
@@ -81,40 +81,48 @@
         friends += [{"tm": mate}]
     for where in friends:
         pl.semaphore_signal(barrier, inc=1, device_id=where, device_id_type=MESH)
-    inputs = [(pattern_hbm, pattern), (factors_hbm, factors), (coul_hbm, pweights.at[0]),
+    plane_rows = [pl.ds(pl.multiple_of(h * R2, R2), R2) for h in (plane, 1 - plane)]
+    inputs = [(pattern_hbm, pattern), (factors_hbm.at[plane_rows[0]], factors.at[0]),
+              (factors_hbm.at[plane_rows[1]], factors.at[1]), (coul_hbm, pweights.at[0]),
               (halves_hbm, weights.at[0, 0])]
     inputs = [pltpu.make_async_copy(src, dst, isem.at[n]) for n, (src, dst) in enumerate(inputs)]
     for copy in inputs + loads:
         copy.start()
-    for copy in inputs:
-        copy.wait()
 
     brows = R // pattern.shape[0]
     bcols = O // pattern.shape[1]
     step = min(brows, R2)
-    for r0 in range(0, R, step):
-        for j in range(pattern.shape[1]):
-            rs, cs = pl.ds(r0, step), pl.ds(j * bcols, bcols)
-            part = (factors[rs, cs].astype(F32) * pattern[r0 // brows, j].astype(F32)).astype(BF16)
-            to = pl.ds(r0 % R2, step)
-            pm[0, r0 // R2, to, cs] = part
-            rows[0, r0 // R2, 0, to, cs] = part
-    pl.semaphore_wait(barrier, len(friends))
+
+    def mask(n, half):
+        inputs[1 + n].wait()
+        for r0 in range(0, R2, step):
+            for j in range(pattern.shape[1]):
+                rs, cs = pl.ds(r0, step), pl.ds(j * bcols, bcols)
+                there = pattern[lax.div(half * R2 + r0, brows), j].astype(F32)
+                part = (factors[n, rs, cs].astype(F32) * there).astype(BF16)
+                pm[0, half, rs, cs] = part
+                rows[0, half, 0, rs, cs] = part
 
     def cut(i):
         return pl.ds(i * PR, PR)
 
     zc, yc, sc, wc, pwc, mc, pc, fc = {}, {}, {}, {}, {}, {}, {}, {}
 
+    inputs[0].wait()
+    mask(0, plane)
+    pl.semaphore_wait(barrier, len(friends))
     for i in range(HP):
         zc[1, 0, i] = send(pm.at[0, plane, cut(i)], rows.at[1, plane, 0, cut(i)],
                            z_s.at[1, 0, i], z_r.at[1, 0, i], aux=nextd)
-    for e in range(1, X):
-        for h in range(2):
-            mc[e, h] = send(pm.at[0, h], pm.at[X - e, h], m_s.at[e, h], m_r.at[e, h],
+    for n, half in enumerate((plane, 1 - plane)):
+        if n:
+            mask(n, half)
+        for e in range(1, X):
+            mc[e, n] = send(pm.at[0, half], pm.at[X - e, half], m_s.at[e, n], m_r.at[e, n],
                             aux=dev(z, xo(e), c))
-    for h in range(2):
-        sc[0, h, 0] = send(pm.at[0, h], rows.at[0, h, 1], s_s.at[0, h, 0], s_r.at[0, h, 0], aux=sibling)
+        sc[0, n, 0] = send(pm.at[0, half], rows.at[0, half, 1], s_s.at[0, n, 0], s_r.at[0, n, 0], aux=sibling)
+    inputs[3].wait()
+    inputs[4].wait()
     for e in range(1, X):
         pwc[e] = send(pweights.at[0], pweights.at[X - e], pw_s.at[e], pw_r.at[e], aux=dev(z, xo(e), c))
     for k in range(Z):
@@ -215,7 +223,7 @@
 
     def need(k, w):
         if k == 0:
-            once(sc[0, w, 0])
+            once(sc[0, 0, 0], sc[0, 1, 0])
         else:
             for i in range(HP):
                 once(sc[k, w, i])
@@ -241,22 +249,6 @@
                 kern[u, 1, to, at] = (w_ * bx).astype(BF16)
             return carry
         lax.fori_loop(0, U * (pn // g), one, 0)
-
-    def early_carried(u, typ):
-        def one(j, carry):
-            at = pl.ds(pl.multiple_of(j * 256, 256), 256)
-            value = None
-            for k in range(Z):
-                if k in (0, 2):
-                    mine, part = pl.ds(2 * k * R, 2 * R), rows[k, :, :, :, at].reshape(2 * R, 256)
-                else:
-                    mine = pl.ds(pl.multiple_of((k * 2 + plane) * R, R), R)
-                    part = rows[k, plane, :, :, at].reshape(R, 256)
-                term = dot(kern[u, typ, pl.ds(0, R), mine], part, 1, 0)
-                value = term if value is None else value + term
-            acc[u, typ, :, at] = value
-            return carry
-        lax.fori_loop(0, O // 256, one, 0)
 
     todo = []
 
@@ -290,10 +282,6 @@
     plan(19.8, tiles, 0, 2, 3, 0)
     plan(20.7, tiles, 0, 2, 2, 1)
 
-    for u in range(U):
-        plan(21.4, early_carried, u, 1)
-        plan(21.4 + 0.9, early_carried, u, 0)
-
     def got(h):
         for u in range(U):
             for e in range(1, X):
@@ -317,10 +305,7 @@
         return pl.ds(pl.multiple_of((k * 2 + half) * R, R), R)
 
     def carried(u, typ, at, width):
-        late = 1 - plane
-        near = acc[u, typ, :, at]
-        for k in (1, Z - 1):
-            near = near + dot(kern[u, typ, pl.ds(0, R), column(k, late)], rows[k, late, :, :, at].reshape(R, width), 1, 0)
+        near = dot(kern[u, typ, pl.ds(0, R)], rows[:, :, :, :, at].reshape(Z * 2 * R, width), 1, 0)
         far = dot(kern[u, typ, pl.ds(R, (X - 1) * R)], rows[:, :, :, :, at].reshape(Z * 2 * R, width), 1, 0)
         return jnp.concatenate([near.astype(BF16), far.astype(BF16)], axis=0)
 
@@ -462,17 +447,17 @@
     dma = pltpu.SemaphoreType.DMA
     vm = pltpu.VMEM
     scratch = [
-        pltpu.SMEM(pattern.shape, jnp.int32), vm((R, O), BF16), vm((T, OUT, O), F32),
+        pltpu.SMEM(pattern.shape, jnp.int32), vm((2, R2, O), BF16), vm((T, OUT, O), F32),
         vm((X, 2, R2, O), BF16), vm((Z, 2, 2, R2, O), BF16), vm((Z, 2, 2, 1, R2), F32),
         vm((X, 1, R), F32), vm((T, O, O), BF16), vm((U, 2, R2, O), BF16),
         vm((U, 2 * X, 2, R2, O), BF16), vm((2 * X, R2, R), F32),
-        vm((U, 2, X * R, Z * 2 * R), BF16), vm((U + 1, X * R, O), BF16), vm((U, 2, R, O), F32), vm((Q, CH, O), F32),
+        vm((U, 2, X * R, Z * 2 * R), BF16), vm((U + 1, X * R, O), BF16), vm((Q, CH, O), F32),
         vm((Q, X, OUT, O), BF16), vm((Q, X, OUT, O), BF16),
         vm((Q, X - 1, OUT, O), BF16), vm((Q, X - 1, OUT, O), BF16),
         vm((Q, OUT, O), BF16), vm((U, 2, 3, OUT, O), BF16), vm((U, 2, OUT, O), BF16),
         vm((U, 2, X, OUT, O), BF16), vm((U, 2, X, OUT, O), BF16),
         vm((U, OUT, O), BF16), vm((U, OUT, O), BF16), vm((U, 2, OUT, O), F32),
-        dma((T,)), dma((4,)), dma((T,)),
+        dma((T,)), dma((5,)), dma((T,)),
         dma((Z, 2, HP)), dma((Z, 2, HP)), dma((Z, HP)), dma((Z, HP)),
         dma((Z, 2, HP)), dma((Z, 2, HP)), dma((Z, 2)), dma((Z, 2)), dma((X,)), dma((X,)),
         dma((X, 2)), dma((X, 2)), dma((U, 2, HP)), dma((U, 2, HP)),

time: 67.7 us -> 66.4 us (0.981)
  Pallas kernels: 65 us -> 63.7 us
    pallas_call x1, Pallas kernels: 65 us -> 63.7 us  [local(): pl.pallas_call(functools.partial(kernel, (Z, X, HP)), out_shape=jax.Shape...]
where the time goes in v4:
time: 66.4 us; the launch traced here: 66.2 us
  Pallas kernels  63.7 us (96%)
  local copies, waits for them, and re-layouts  2.56 us (4%)
    pallas_call x1, Pallas kernels, local(): pl.pallas_call(functools.partial(kernel, (Z, X, HP)), out_shape=jax.Shape...  63.7 us
    unnamed x4, local copies, waits for them, and re-layouts  1.36 us

profile of v4, /device:TPU:0, one launch (start us, length us, event | category | flops | bytes accessed | tf_op | source)
XLA Modules:
  0.0 66.2 jit_solution(7711005512628153384)
XLA Ops:
  0.0 0.0 copy-start
  0.0 0.7 %copy-done = f32[256]{0:T(256)S(1)} copy-done((f32[256]{0:T(256)S(1)}, f32[256]{0:T(256)}, u32[]{:S(2)}) %copy-start) | copy-done | bytes 1048
  0.7 0.0 copy-start.1
  0.7 0.7 %copy-done.1 = s32[2,8]{1,0:T(2,128)S(1)} copy-done((s32[2,8]{1,0:T(2,128)S(1)}, s32[2,8]{1,0:T(2,128)}, u32[]{:S(2)}) %copy-start.1) | copy-done | bytes 88
  1.4 63.7 %shard_map.46 = f32[2,64,1024]{2,1,0:T(8,128)S(1)} custom-call(s32[2,8]{1,0:T(2,128)S(1)} %copy-done.1, bf16[256,1024]{1,0:T(8,128)(2,1)} %factors_hbm.1, f32[1,256]{1,0:T(1,128)S(1)} %bitcast.4, f32[2,1,128]{2,1,0:T(1,128)S(1)} %bitcast.5, bf16[2,1024,1024]{2,1,0:T(8,128)(2,1)} %green_hbm.1), custom_call_target="tpu_custom_call" | custom-call | tf_op jit(solution)/shard_map/pallas_call | solution.py:469
  65.0 1.2 %copy.5 = f32[64,2,1024]{2,1,0:T(2,128)} copy(f32[64,2,1024]{2,0,1:T(8,128)S(1)} %bitcast.3) | data formatting | bytes 1048576 | tf_op jit(solution)/shard_map/transpose | solution.py:478
Async XLA Ops:
  0.0 0.7 %copy-start = (f32[256]{0:T(256)S(1)}, f32[256]{0:T(256)}, u32[]{:S(2)}) copy-start(f32[256]{0:T(256)} %param.7) | copy-start | bytes 3076
  0.7 0.7 %copy-start.1 = (s32[2,8]{1,0:T(2,128)S(1)}, s32[2,8]{1,0:T(2,128)}, u32[]{:S(2)}) copy-start(s32[2,8]{1,0:T(2,128)} %pattern_hbm.1) | copy-start | bytes 196

commit v5 on v4

--- a/solution.py
+++ b/solution.py
@@ -417,7 +417,7 @@
         ("A", 1, DIAG), ("A", 1, NB), ("B", 1, DIAG), ("A", 1, CROSS), ("G", 1, 0), ("W", 0),
         ("B", 1, CROSS), ("W", 1), ("W", 2), ("W", 3), ("A", 0, DIAG), ("C", 1, DIAG),
         ("G", 1, 1), ("A", 0, CROSS), ("B", 0, DIAG), ("B", 0, CROSS), ("A", 1, OWN), ("A", 0, NB),
-        ("C", 1, CROSS), ("B", 0, NB), ("A", 0, OWN), ("B", 1, OWN), ("C", 0, DIAG), ("C", 0, CROSS),
+        ("B", 0, NB), ("C", 1, CROSS), ("C", 0, DIAG), ("A", 0, OWN), ("B", 1, OWN), ("C", 0, CROSS),
         ("B", 0, OWN), ("C", 0, NB), ("C", 1, OWN), ("D", 1), ("C", 0, OWN), ("E",),
         ("D", 0),
     )

time: 66.4 us -> 66.4 us (level)
  no operation moved by 1% of the time
where the time goes in v5:
time: 66.4 us; the launch traced here: 66.3 us
  Pallas kernels  63.7 us (96%)
  local copies, waits for them, and re-layouts  2.56 us (4%)
    pallas_call x1, Pallas kernels, local(): pl.pallas_call(functools.partial(kernel, (Z, X, HP)), out_shape=jax.Shape...  63.7 us
    unnamed x4, local copies, waits for them, and re-layouts  1.36 us

profile of v5, /device:TPU:0, one launch (start us, length us, event | category | flops | bytes accessed | tf_op | source)
XLA Modules:
  0.0 66.3 jit_solution(12348777752746924542)
XLA Ops:
  0.0 0.0 copy-start
  0.0 0.7 %copy-done = f32[256]{0:T(256)S(1)} copy-done((f32[256]{0:T(256)S(1)}, f32[256]{0:T(256)}, u32[]{:S(2)}) %copy-start) | copy-done | bytes 1048
  0.7 0.0 copy-start.1
  0.7 0.7 %copy-done.1 = s32[2,8]{1,0:T(2,128)S(1)} copy-done((s32[2,8]{1,0:T(2,128)S(1)}, s32[2,8]{1,0:T(2,128)}, u32[]{:S(2)}) %copy-start.1) | copy-done | bytes 88
  1.4 63.7 %shard_map.46 = f32[2,64,1024]{2,1,0:T(8,128)S(1)} custom-call(s32[2,8]{1,0:T(2,128)S(1)} %copy-done.1, bf16[256,1024]{1,0:T(8,128)(2,1)} %factors_hbm.1, f32[1,256]{1,0:T(1,128)S(1)} %bitcast.4, f32[2,1,128]{2,1,0:T(1,128)S(1)} %bitcast.5, bf16[2,1024,1024]{2,1,0:T(8,128)(2,1)} %green_hbm.1), custom_call_target="tpu_custom_call" | custom-call | tf_op jit(solution)/shard_map/pallas_call | solution.py:469
  65.1 1.2 %copy.5 = f32[64,2,1024]{2,1,0:T(2,128)} copy(f32[64,2,1024]{2,0,1:T(8,128)S(1)} %bitcast.3) | data formatting | bytes 1048576 | tf_op jit(solution)/shard_map/transpose | solution.py:478
Async XLA Ops:
  0.0 0.7 %copy-start = (f32[256]{0:T(256)S(1)}, f32[256]{0:T(256)}, u32[]{:S(2)}) copy-start(f32[256]{0:T(256)} %param.7) | copy-start | bytes 3076
  0.7 0.7 %copy-start.1 = (s32[2,8]{1,0:T(2,128)S(1)}, s32[2,8]{1,0:T(2,128)}, u32[]{:S(2)}) copy-start(s32[2,8]{1,0:T(2,128)} %pattern_hbm.1) | copy-start | bytes 196
